TPU v7x, 512 devices: a whole 4x8x8 slice. The times are simulated.
512 devices in a mesh: ctx: 32 (over z_hi, y, core), tp: 16 (over z_lo, x).
Axes of the slice: x: 4, y: 8, z: 8 (z_hi: 2, z_lo: 4; z = z_hi * 4 + z_lo), core: 2. Of those that a mesh axis runs over, the one named last changes fastest.
Arguments:
- enc_query: bfloat16 [5120, 6144], P(('ctx', 'tp')), may hold values from -40 to 40
- enc_key: bfloat16 [5120, 6144], P(('ctx', 'tp')), may hold values from -5 to 5
- enc_value: bfloat16 [5120, 6144], P(('ctx', 'tp')), may hold values from -6 to 6
- dec_query: bfloat16 [1024, 6144], P(('ctx', 'tp')), may hold values from -40 to 40
- cross_key: bfloat16 [5120, 6144], P(('ctx', 'tp')), may hold values from -5 to 5
- cross_value: bfloat16 [5120, 6144], P(('ctx', 'tp')), may hold values from -6 to 6
Outputs:
- enc_context: bfloat16 [5120, 6144], P('ctx', 'tp')
- dec_context: bfloat16 [1024, 6144], P('ctx', 'tp')
All inputs are finite; a program needn't handle non-finite values.
Results may differ from a plain program's by a relative error of at most 0.004.
Values may be sent and summed in bfloat16 or wider, within the bound.
A program may use at most 64 MiB of HBM per device.

v0:
```python
import jax
import jax.numpy as jnp
from jax import lax
from jax.sharding import PartitionSpec as P

HEAD_DIM = 128


def absorb(partial_state, query_block, key_block, value_block):
    row_top, row_total, weighted = partial_state
    head_count = query_block.shape[1] // HEAD_DIM
    query_heads = query_block.reshape(query_block.shape[0], head_count, HEAD_DIM)
    key_heads = key_block.reshape(key_block.shape[0], head_count, HEAD_DIM)
    value_heads = value_block.reshape(value_block.shape[0], head_count, HEAD_DIM)
    scores = jnp.einsum(
        "qhd,khd->hqk", query_heads, key_heads, preferred_element_type=jnp.float32
    ) * HEAD_DIM ** (-0.5)
    new_top = jnp.maximum(row_top, jnp.max(scores, axis=2))
    shrink = jnp.exp(row_top - new_top)
    weights = jnp.exp(scores - new_top[:, :, None])
    row_total = row_total * shrink + jnp.sum(weights, axis=2)
    mixed_values = jnp.einsum(
        "hqk,khd->qhd",
        weights.astype(jnp.bfloat16),
        value_heads,
        preferred_element_type=jnp.float32,
    )
    weighted = weighted * jnp.transpose(shrink)[:, :, None] + mixed_values
    return (new_top, row_total, weighted)


def empty_state(row_count, columns):
    head_count = columns // HEAD_DIM
    return (
        jnp.full((head_count, row_count), -1e30, jnp.float32),
        jnp.zeros((head_count, row_count), jnp.float32),
        jnp.zeros((row_count, head_count, HEAD_DIM), jnp.float32),
    )


def finish(partial_state):
    row_top, row_total, weighted = partial_state
    normed = weighted / jnp.transpose(row_total)[:, :, None]
    return normed.reshape(weighted.shape[0], -1).astype(jnp.bfloat16)


def shards(enc_query, enc_key, enc_value, dec_query, cross_key, cross_value):
    local_query, local_key, local_value, visitor, resident_key, resident_value = (
        lax.all_to_all(enc_query, "tp", split_axis=1, concat_axis=0, tiled=True),
        lax.all_to_all(enc_key, "tp", split_axis=1, concat_axis=0, tiled=True),
        lax.all_to_all(enc_value, "tp", split_axis=1, concat_axis=0, tiled=True),
        lax.all_to_all(dec_query, "tp", split_axis=1, concat_axis=0, tiled=True),
        lax.all_to_all(cross_key, "tp", split_axis=1, concat_axis=0, tiled=True),
        lax.all_to_all(cross_value, "tp", split_axis=1, concat_axis=0, tiled=True),
    )
    enc_state = absorb(
        empty_state(local_query.shape[0], local_query.shape[1]),
        local_query,
        lax.all_gather(local_key, "ctx", axis=0, tiled=True),
        lax.all_gather(local_value, "ctx", axis=0, tiled=True),
    )
    enc_context = finish(enc_state)
    ring = lax.axis_size("ctx")
    rows, columns = visitor.shape
    heads = columns // HEAD_DIM
    every_query = lax.all_gather(visitor, "ctx", axis=0, tiled=True)
    row_top, row_total, weighted = absorb(
        empty_state(rows * ring, columns), every_query, resident_key, resident_value
    )
    stats = jnp.stack([row_top.T, row_total.T], axis=1).reshape(ring, rows, 2 * heads)
    sums = weighted.reshape(ring, rows, columns).astype(jnp.bfloat16)
    stats = lax.all_to_all(stats, "ctx", split_axis=0, concat_axis=0, tiled=True)
    sums = lax.all_to_all(sums, "ctx", split_axis=0, concat_axis=0, tiled=True)
    stats = stats.reshape(ring, rows, 2, heads)
    tops, totals = (stats[:, :, 0], stats[:, :, 1])
    scale = jnp.exp(tops - jnp.max(tops, axis=0, keepdims=True))
    total = jnp.sum(scale * totals, axis=0)
    mixed = jnp.sum(
        scale[..., None] * sums.reshape(ring, rows, heads, HEAD_DIM).astype(jnp.float32), axis=0
    )
    dec_context = (mixed / total[..., None]).reshape(rows, columns).astype(jnp.bfloat16)
    return (enc_context, dec_context)


def solution(mesh):
    in_specs = (
        P(("ctx", "tp"), None),
        P(("ctx", "tp"), None),
        P(("ctx", "tp"), None),
        P(("ctx", "tp"), None),
        P(("ctx", "tp"), None),
        P(("ctx", "tp"), None),
    )
    out_specs = (P("ctx", "tp"), P("ctx", "tp"))
    return jax.shard_map(shards, mesh=mesh, in_specs=in_specs, out_specs=out_specs, check_vma=False)
```

profile of v0, /device:TPU:1, one launch (start us, length us, event | category | flops | bytes accessed | tf_op | source)
XLA Modules:
  0.0 264.9 jit_solution(9463373634563402771)
XLA Ops:
  8.3 18.6 %all_to_all.115 = bf16[10,16,384]{2,0,1:T(8,128)(2,1)S(1)} all-to-all(bf16[10,16,384]{2,0,1:T(8,128)(2,1)S(1)} %copy.50), channel_id=1, replica_groups=mesh['ctx'=32,'tp'=16] {'tp'}, dimensions={1} | all-to-all | bytes 245760 | tf_op jit(solution)/shard_map/all_to_all | solution.py:50
  28.7 12.5 %all_to_all.116 = bf16[10,16,384]{2,0,1:T(8,128)(2,1)S(1)} all-to-all(bf16[10,16,384]{2,0,1:T(8,128)(2,1)S(1)} %copy.54), channel_id=1, replica_groups=mesh['ctx'=32,'tp'=16] {'tp'}, dimensions={1} | all-to-all | bytes 245760 | tf_op jit(solution)/shard_map/all_to_all | solution.py:51
  41.9 4.2 %all-to-all-start.3 = ((bf16[2,16,384]{2,0,1:T(2,128)(2,1)}), bf16[2,16,384]{2,0,1:T(2,128)(2,1)S(1)}, u32[]{:S(2)}, u32[]{:S(2)}) async-start(bf16[2,16,384]{2,0,1:T(2,128)(2,1)} %bitcast.118), calls=%async_computation.3 | async-start | bytes 49152 | tf_op jit(solution)/shard_map/all_to_all | solution.py:52
  49.3 3.8 %all-to-all-done.3 = bf16[2,16,384]{2,0,1:T(2,128)(2,1)S(1)} async-done(((bf16[2,16,384]{2,0,1:T(2,128)(2,1)}), bf16[2,16,384]{2,0,1:T(2,128)(2,1)S(1)}, u32[]{:S(2)}, u32[]{:S(2)}) %all-to-all-start.3) | async-done | bytes 24608 | tf_op jit(solution)/shard_map/all_to_all | solution.py:52
  53.1 3.5 %all-to-all-start.4 = ((bf16[10,16,384]{2,0,1:T(8,128)(2,1)}), bf16[10,16,384]{2,0,1:T(8,128)(2,1)S(1)}, u32[]{:S(2)}, u32[]{:S(2)}) async-start(bf16[10,16,384]{2,0,1:T(8,128)(2,1)} %copy.60), calls=%async_computation.4 | async-start | bytes 393216 | tf_op jit(solution)/shard_map/all_to_all | solution.py:53
  56.7 61.8 %all_gather.11 = bf16[1024,384]{1,0:T(8,128)(2,1)S(1)} all-gather(bf16[32,384]{1,0:T(8,128)(2,1)S(1)} %all_to_all.98), channel_id=1, replica_groups=mesh['ctx'=32,'tp'=16] {'ctx'}, dimensions={0}, use_global_device_ids=true | all-gather | bytes 811008 | tf_op jit(solution)/shard_map/all_gather | solution.py:66
  118.8 6.6 %all-to-all-start.6 = ((bf16[10,16,384]{2,0,1:T(8,128)(2,1)}), bf16[10,16,384]{2,0,1:T(8,128)(2,1)S(1)}, u32[]{:S(2)}, u32[]{:S(2)}) async-start(bf16[10,16,384]{2,0,1:T(8,128)(2,1)} %copy.66), calls=%async_computation.6 | async-start | bytes 393216 | tf_op jit(solution)/shard_map/all_to_all | solution.py:54
  126.3 8.1 %all-to-all-done.6 = bf16[10,16,384]{2,0,1:T(8,128)(2,1)S(1)} async-done(((bf16[10,16,384]{2,0,1:T(8,128)(2,1)}), bf16[10,16,384]{2,0,1:T(8,128)(2,1)S(1)}, u32[]{:S(2)}, u32[]{:S(2)}) %all-to-all-start.6) | async-done | bytes 122912 | tf_op jit(solution)/shard_map/all_to_all | solution.py:54
  134.4 3.9 %all-to-all-start = ((bf16[10,16,384]{2,0,1:T(8,128)(2,1)}), bf16[10,16,384]{2,0,1:T(8,128)(2,1)S(1)}, u32[]{:S(2)}, u32[]{:S(2)}) async-start(bf16[10,16,384]{2,0,1:T(8,128)(2,1)} %copy.49), calls=%async_computation | async-start | bytes 393216 | tf_op jit(solution)/shard_map/all_to_all | solution.py:49
  139.3 7.3 %all-to-all-done = bf16[10,16,384]{2,0,1:T(8,128)(2,1)S(1)} async-done(((bf16[10,16,384]{2,0,1:T(8,128)(2,1)}), bf16[10,16,384]{2,0,1:T(8,128)(2,1)S(1)}, u32[]{:S(2)}, u32[]{:S(2)}) %all-to-all-start) | async-done | bytes 122912 | tf_op jit(solution)/shard_map/all_to_all | solution.py:49
  146.6 5.8 %all-to-all-start.5 = ((f32[32,1,192]{2,1,0:T(1,128)}), f32[32,1,192]{2,1,0:T(1,128)S(1)}, u32[]{:S(2)}, u32[]{:S(2)}) async-start(f32[32,1,192]{2,1,0:T(1,128)} %reshape.85), calls=%async_computation.5 | async-start | bytes 65536 | tf_op jit(solution)/shard_map/all_to_all | solution.py:72
  154.1 1.4 convert_element_type.30
  155.5 8.8 %all-to-all-done.5 = f32[32,1,192]{2,1,0:T(1,128)S(1)} async-done(((f32[32,1,192]{2,1,0:T(1,128)}), f32[32,1,192]{2,1,0:T(1,128)S(1)}, u32[]{:S(2)}, u32[]{:S(2)}) %all-to-all-start.5) | async-done | bytes 24608 | tf_op jit(solution)/shard_map/all_to_all | solution.py:72
  164.3 4.6 %all-to-all-start.7 = ((bf16[32,32,384]{2,1,0:T(8,128)(2,1)}), bf16[32,32,384]{2,1,0:T(8,128)(2,1)S(1)}, u32[]{:S(2)}, u32[]{:S(2)}) async-start(bf16[32,32,384]{2,1,0:T(8,128)(2,1)} %convert_element_type.30), calls=%async_computation.7 | async-start | bytes 1572864 | tf_op jit(solution)/shard_map/all_to_all | solution.py:73
  172.6 1.8 mul.42
  174.5 20.3 %all-to-all-done.7 = bf16[32,32,384]{2,1,0:T(8,128)(2,1)S(1)} async-done(((bf16[32,32,384]{2,1,0:T(8,128)(2,1)}), bf16[32,32,384]{2,1,0:T(8,128)(2,1)S(1)}, u32[]{:S(2)}, u32[]{:S(2)}) %all-to-all-start.7) | async-done | bytes 786464 | tf_op jit(solution)/shard_map/all_to_all | solution.py:73
  194.8 1.6 multiply_reduce_fusion.2
  197.1 6.3 %copy.51 = bf16[5120,384]{0,1:T(8,128)(2,1)} copy(bf16[5120,384]{1,0:T(8,128)(2,1)} %all-gather.3.cloned.1.call-done) | data formatting | bytes 7864320 | tf_op jit(solution)/shard_map/all_gather | solution.py:59
  203.4 3.6 %multiply_reduce_fusion = (f32[3,160]{1,0:T(4,128)S(1)}, f32[3,160,5120]{2,1,0:T(8,128)S(1)}) fusion(bf16[5120,3,128]{0,2,1:T(8,128)(2,1)} %bitcast.93, bf16[160,3,128]{2,1,0:T(4,128)(2,1)S(1)} %copy-done.1), kind=kOutput, calls=%fused_computation.1 | convolution fusion | flops 634060288 | bytes 13887360 | tf_op jit(solution)/shard_map/qhd,khd->hqk/dot_general | solution.py:15
  207.1 1.8 fusion
  208.9 2.0 copy-done
  210.9 33.3 %all-gather.5.cloned.1.call-done = bf16[5120,384]{1,0:T(8,128)(2,1)} async-done(((bf16[160,384]{1,0:T(8,128)(2,1)}), bf16[5120,384]{1,0:T(8,128)(2,1)}) %all-gather.5.cloned.1.call-update) | async-done | bytes 3932176 | tf_op jit(solution)/shard_map/all_gather | solution.py:60
  244.2 6.3 %copy.55 = bf16[5120,384]{0,1:T(8,128)(2,1)} copy(bf16[5120,384]{1,0:T(8,128)(2,1)} %all-gather.5.cloned.1.call-done) | data formatting | bytes 7864320 | tf_op jit(solution)/shard_map/all_gather | solution.py:60
  250.5 6.9 %fusion.21 = bf16[3,20,8,128]{3,2,1,0:T(8,128)(2,1)S(1)} fusion(bf16[5120,3,128]{0,2,1:T(8,128)(2,1)} %bitcast.94, f32[3,160,5120]{2,1,0:T(8,128)} %copy-done, f32[3,160]{1,0:T(4,128)S(1)} %get-tuple-element.9, f32[160,3]{0,1:T(4,128)S(1)} %bitcast_add_fusion.2, f32[160,3]{0,1:T(4,128)S(1)} %get-tuple-element.8), kind=kOutput, calls=%fused_computation.18 | convolution fusion | flops 636702720 | bytes 13891200 | tf_op jit(solution)/shard_map/hqk,khd->qhd/dot_general | solution.py:22
  (59 shorter events, 15.8 us)
Async XLA Ops:
  7.2 40.6 %copy-start.2 = (bf16[10,6144]{1,0:T(8,128)(2,1)S(1)}, bf16[10,6144]{1,0:T(8,128)(2,1)}, u32[]{:S(2)}) copy-start(bf16[10,6144]{1,0:T(8,128)(2,1)} %param.11) | copy-start | bytes 368644
  7.2 41.4 %copy-start.3 = (bf16[10,6144]{1,0:T(8,128)(2,1)S(1)}, bf16[10,6144]{1,0:T(8,128)(2,1)}, u32[]{:S(2)}) copy-start(bf16[10,6144]{1,0:T(8,128)(2,1)} %param.6) | copy-start | bytes 368644
  7.2 189.9 %all-gather.3.cloned.1.call-start = ((), (), s32[]{:S(2)}) async-start(), calls=%async_computation.8 | async-start | bytes 4055040 | tf_op jit(solution)/shard_map/all_gather | solution.py:59
  27.7 216.5 %all-gather.5.cloned.1.call-start = ((), (), s32[]{:S(2)}) async-start(), calls=%async_computation.9 | async-start | bytes 4055040 | tf_op jit(solution)/shard_map/all_gather | solution.py:60
  41.9 11.2 %all-to-all-start.3 = ((bf16[2,16,384]{2,0,1:T(2,128)(2,1)}), bf16[2,16,384]{2,0,1:T(2,128)(2,1)S(1)}, u32[]{:S(2)}, u32[]{:S(2)}) async-start(bf16[2,16,384]{2,0,1:T(2,128)(2,1)} %bitcast.118), calls=%async_computation.3 | async-start | bytes 49152 | tf_op jit(solution)/shard_map/all_to_all | solution.py:52
  53.1 65.7 %all-to-all-start.4 = ((bf16[10,16,384]{2,0,1:T(8,128)(2,1)}), bf16[10,16,384]{2,0,1:T(8,128)(2,1)S(1)}, u32[]{:S(2)}, u32[]{:S(2)}) async-start(bf16[10,16,384]{2,0,1:T(8,128)(2,1)} %copy.60), calls=%async_computation.4 | async-start | bytes 393216 | tf_op jit(solution)/shard_map/all_to_all | solution.py:53
  118.8 15.6 %all-to-all-start.6 = ((bf16[10,16,384]{2,0,1:T(8,128)(2,1)}), bf16[10,16,384]{2,0,1:T(8,128)(2,1)S(1)}, u32[]{:S(2)}, u32[]{:S(2)}) async-start(bf16[10,16,384]{2,0,1:T(8,128)(2,1)} %copy.66), calls=%async_computation.6 | async-start | bytes 393216 | tf_op jit(solution)/shard_map/all_to_all | solution.py:54
  134.4 12.2 %all-to-all-start = ((bf16[10,16,384]{2,0,1:T(8,128)(2,1)}), bf16[10,16,384]{2,0,1:T(8,128)(2,1)S(1)}, u32[]{:S(2)}, u32[]{:S(2)}) async-start(bf16[10,16,384]{2,0,1:T(8,128)(2,1)} %copy.49), calls=%async_computation | async-start | bytes 393216 | tf_op jit(solution)/shard_map/all_to_all | solution.py:49
  146.6 17.8 %all-to-all-start.5 = ((f32[32,1,192]{2,1,0:T(1,128)}), f32[32,1,192]{2,1,0:T(1,128)S(1)}, u32[]{:S(2)}, u32[]{:S(2)}) async-start(f32[32,1,192]{2,1,0:T(1,128)} %reshape.85), calls=%async_computation.5 | async-start | bytes 65536 | tf_op jit(solution)/shard_map/all_to_all | solution.py:72
  164.3 30.5 %all-to-all-start.7 = ((bf16[32,32,384]{2,1,0:T(8,128)(2,1)}), bf16[32,32,384]{2,1,0:T(8,128)(2,1)S(1)}, u32[]{:S(2)}, u32[]{:S(2)}) async-start(bf16[32,32,384]{2,1,0:T(8,128)(2,1)} %convert_element_type.30), calls=%async_computation.7 | async-start | bytes 1572864 | tf_op jit(solution)/shard_map/all_to_all | solution.py:73
  197.1 6.3 %copy-start.1 = (bf16[160,3,128]{2,1,0:T(4,128)(2,1)S(1)}, bf16[160,3,128]{2,1,0:T(4,128)(2,1)}, u32[]{:S(2)}) copy-start(bf16[160,3,128]{2,1,0:T(4,128)(2,1)} %reshape.77) | copy-start | bytes 368644
  207.1 3.8 %copy-start = (f32[3,160,5120]{2,1,0:T(8,128)}, f32[3,160,5120]{2,1,0:T(8,128)S(1)}, u32[]{:S(2)}) copy-start(f32[3,160,5120]{2,1,0:T(8,128)S(1)} %get-tuple-element.11) | copy-start | bytes 29491204
Sparse Core Ops, SparseCore 0:
  27.8 109.4 all-gather.2
  141.2 102.8 all-gather.4
where the time goes:
time: 266 us; the launch traced here: 265 us
  blocking collectives  92.9 us (35%)
  waiting for transfers between devices  81.7 us (31%)
  local copies, waits for them, and re-layouts  30.2 us (11%)
  starting transfers between devices  28.6 us (11%)
  between operations  14.3 us (5%)
  matrix products  12 us (5%)
  other arithmetic  5.18 us (2%)
    all_gather x1, blocking collectives, shards(): every_query = lax.all_gather(visitor, 'ctx', axis=0, tiled=True)  61.8 us
    all_gather x1, waiting for transfers between devices, shards(): lax.all_gather(local_value, 'ctx', axis=0, tiled=True)  33.3 us
    all_to_all x1, waiting for transfers between devices, shards(): sums = lax.all_to_all(sums, 'ctx', split_axis=0, concat_axis=0, tiled=True)  20.3 us
    all_to_all x1, blocking collectives, shards(): lax.all_to_all(enc_key, 'tp', split_axis=1, concat_axis=0, tiled=True)  18.6 us
    all_to_all x1, blocking collectives, shards(): lax.all_to_all(enc_value, 'tp', split_axis=1, concat_axis=0, tiled=True)  12.5 us
    all_to_all x1, waiting for transfers between devices, shards(): lax.all_to_all(stats, 'ctx', split_axis=0, concat_axis=0, tiled=True)  8.81 us
    all_to_all x1, waiting for transfers between devices, shards(): lax.all_to_all(cross_value, 'tp', split_axis=1, concat_axis=0, tiled=True)  8.13 us
    dot_general x2, matrix products, absorb(): jnp.einsum('hqk,khd->qhd', weights.astype(jnp.bfloat16), value_heads, pre...  7.91 us
  transfers between devices with their start and end apart: 8, of which 6 were waited for; matrix products, arithmetic and copies ran while one was open for 11% of the time, Pallas kernels for 0%

commit v1 on v0

--- a/solution.py
+++ b/solution.py
@@ -4,6 +4,13 @@
 from jax.sharding import PartitionSpec as P
 
 HEAD_DIM = 128
+
+
+def lead_slices(w_in, named_axis):
+    local_next = lax.all_to_all(
+        jnp.stack(tuple((w_in for _ in range(lax.psum(1, named_axis)))), axis=0), named_axis, 0, 0
+    )
+    return jnp.concatenate(local_next, axis=0)
 
 
 def absorb(partial_state, query_block, key_block, value_block):
@@ -63,7 +70,7 @@
     ring = lax.axis_size("ctx")
     rows, columns = visitor.shape
     heads = columns // HEAD_DIM
-    every_query = lax.all_gather(visitor, "ctx", axis=0, tiled=True)
+    every_query = lead_slices(visitor, "ctx")
     row_top, row_total, weighted = absorb(
         empty_state(rows * ring, columns), every_query, resident_key, resident_value
     )

time: 266 us -> 286 us (1.075)
  blocking collectives: 92.9 us -> 31.2 us
  waiting for transfers between devices: 81.7 us -> 143 us
  starting transfers between devices: 28.6 us -> 47.6 us
    all_gather x1 -> x0, blocking collectives: 61.8 us -> none  [shards(): every_query = lax.all_gather(visitor, 'ctx', axis=0, tiled=True)]
    all_gather x1, waiting for transfers between devices: 33.3 us -> 59.5 us  [shards(): lax.all_gather(local_value, 'ctx', axis=0, tiled=True)]
    all_to_all x0 -> x1, waiting for transfers between devices: none -> 24.9 us  [lead_slices(): lax.all_to_all(jnp.stack(tuple((w_in for _ in range(lax.psum(1, named_axi...]
    all_to_all x0 -> x1, starting transfers between devices: none -> 18 us  [lead_slices(): lax.all_to_all(jnp.stack(tuple((w_in for _ in range(lax.psum(1, named_axi...]
    all_to_all x1, waiting for transfers between devices: 0.01 us -> 7.51 us  [shards(): lax.all_to_all(cross_key, 'tp', split_axis=1, concat_axis=0, tiled=True)]
    all_to_all x1, starting transfers between devices: 5.8 us -> 9.07 us  [shards(): lax.all_to_all(stats, 'ctx', split_axis=0, concat_axis=0, tiled=True)]
    all_to_all x1, starting transfers between devices: 6.58 us -> 3.52 us  [shards(): lax.all_to_all(cross_value, 'tp', split_axis=1, concat_axis=0, tiled=True)]
  transfers between devices with their start and end apart: 8 -> 9, of which waited for: 6 -> 8; matrix products, arithmetic and copies ran while one was open for 11% -> 11% of each run, Pallas kernels for 0% -> 0%
where the time goes in v1:
time: 286 us; the launch traced here: 284 us
  waiting for transfers between devices  143 us (50%)
  starting transfers between devices  47.6 us (17%)
  local copies, waits for them, and re-layouts  31.2 us (11%)
  blocking collectives  31.2 us (11%)
  between operations  14.4 us (5%)
  matrix products  12 us (4%)
  other arithmetic  5.18 us (2%)
    all_gather x1, waiting for transfers between devices, shards(): lax.all_gather(local_value, 'ctx', axis=0, tiled=True)  59.5 us
    all_to_all x1, waiting for transfers between devices, lead_slices(): lax.all_to_all(jnp.stack(tuple((w_in for _ in range(lax.psum(1, named_axi...  24.9 us
    all_to_all x1, waiting for transfers between devices, shards(): sums = lax.all_to_all(sums, 'ctx', split_axis=0, concat_axis=0, tiled=True)  22.4 us
    all_to_all x1, blocking collectives, shards(): lax.all_to_all(enc_key, 'tp', split_axis=1, concat_axis=0, tiled=True)  18.7 us
    all_to_all x1, starting transfers between devices, lead_slices(): lax.all_to_all(jnp.stack(tuple((w_in for _ in range(lax.psum(1, named_axi...  18 us
    all_to_all x1, blocking collectives, shards(): lax.all_to_all(enc_value, 'tp', split_axis=1, concat_axis=0, tiled=True)  12.5 us
    all_to_all x1, starting transfers between devices, shards(): lax.all_to_all(stats, 'ctx', split_axis=0, concat_axis=0, tiled=True)  9.07 us
    all_to_all x1, waiting for transfers between devices, shards(): lax.all_to_all(stats, 'ctx', split_axis=0, concat_axis=0, tiled=True)  8.69 us
  transfers between devices with their start and end apart: 9, of which 8 were waited for; matrix products, arithmetic and copies ran while one was open for 11% of the time, Pallas kernels for 0%

profile of v1, /device:TPU:1, one launch (start us, length us, event | category | flops | bytes accessed | tf_op | source)
XLA Modules:
  0.0 284.5 jit_solution(14197736209707425150)
XLA Ops:
  8.3 18.7 %all_to_all.117 = bf16[10,16,384]{2,0,1:T(8,128)(2,1)S(1)} all-to-all(bf16[10,16,384]{2,0,1:T(8,128)(2,1)S(1)} %copy.48), channel_id=1, replica_groups=mesh['ctx'=32,'tp'=16] {'tp'}, dimensions={1} | all-to-all | bytes 245760 | tf_op jit(solution)/shard_map/all_to_all | solution.py:57
  28.8 12.5 %all_to_all.118 = bf16[10,16,384]{2,0,1:T(8,128)(2,1)S(1)} all-to-all(bf16[10,16,384]{2,0,1:T(8,128)(2,1)S(1)} %copy.52), channel_id=1, replica_groups=mesh['ctx'=32,'tp'=16] {'tp'}, dimensions={1} | all-to-all | bytes 245760 | tf_op jit(solution)/shard_map/all_to_all | solution.py:58
  42.0 4.2 %all-to-all-start.3 = ((bf16[2,16,384]{2,0,1:T(2,128)(2,1)}), bf16[2,16,384]{2,0,1:T(2,128)(2,1)S(1)}, u32[]{:S(2)}, u32[]{:S(2)}) async-start(bf16[2,16,384]{2,0,1:T(2,128)(2,1)} %bitcast.115), calls=%async_computation.3 | async-start | bytes 49152 | tf_op jit(solution)/shard_map/all_to_all | solution.py:59
  47.9 5.4 %all-to-all-done.3 = bf16[2,16,384]{2,0,1:T(2,128)(2,1)S(1)} async-done(((bf16[2,16,384]{2,0,1:T(2,128)(2,1)}), bf16[2,16,384]{2,0,1:T(2,128)(2,1)S(1)}, u32[]{:S(2)}, u32[]{:S(2)}) %all-to-all-start.3) | async-done | bytes 24608 | tf_op jit(solution)/shard_map/all_to_all | solution.py:59
  53.2 3.5 %all-to-all-start.5 = ((bf16[10,16,384]{2,0,1:T(8,128)(2,1)}), bf16[10,16,384]{2,0,1:T(8,128)(2,1)S(1)}, u32[]{:S(2)}, u32[]{:S(2)}) async-start(bf16[10,16,384]{2,0,1:T(8,128)(2,1)} %copy.57), calls=%async_computation.5 | async-start | bytes 393216 | tf_op jit(solution)/shard_map/all_to_all | solution.py:60
  57.5 7.5 %all-to-all-done.5 = bf16[10,16,384]{2,0,1:T(8,128)(2,1)S(1)} async-done(((bf16[10,16,384]{2,0,1:T(8,128)(2,1)}), bf16[10,16,384]{2,0,1:T(8,128)(2,1)S(1)}, u32[]{:S(2)}, u32[]{:S(2)}) %all-to-all-start.5) | async-done | bytes 122912 | tf_op jit(solution)/shard_map/all_to_all | solution.py:60
  65.0 3.5 %all-to-all-start.7 = ((bf16[10,16,384]{2,0,1:T(8,128)(2,1)}), bf16[10,16,384]{2,0,1:T(8,128)(2,1)S(1)}, u32[]{:S(2)}, u32[]{:S(2)}) async-start(bf16[10,16,384]{2,0,1:T(8,128)(2,1)} %copy.63), calls=%async_computation.7 | async-start | bytes 393216 | tf_op jit(solution)/shard_map/all_to_all | solution.py:61
  68.6 8.2 %all-to-all-done.7 = bf16[10,16,384]{2,0,1:T(8,128)(2,1)S(1)} async-done(((bf16[10,16,384]{2,0,1:T(8,128)(2,1)}), bf16[10,16,384]{2,0,1:T(8,128)(2,1)S(1)}, u32[]{:S(2)}, u32[]{:S(2)}) %all-to-all-start.7) | async-done | bytes 122912 | tf_op jit(solution)/shard_map/all_to_all | solution.py:61
  77.8 18.0 %all-to-all-start.4 = ((bf16[32,32,384]{2,1,0:T(8,128)(2,1)}), bf16[32,32,384]{2,1,0:T(8,128)(2,1)S(1)}, u32[]{:S(2)}, u32[]{:S(2)}) async-start(bf16[32,32,384]{2,1,0:T(8,128)(2,1)} %stack.11), calls=%async_computation.4 | async-start | bytes 1572864 | tf_op jit(solution)/shard_map/all_to_all | solution.py:10
  96.7 24.9 %all-to-all-done.4 = bf16[32,32,384]{2,1,0:T(8,128)(2,1)S(1)} async-done(((bf16[32,32,384]{2,1,0:T(8,128)(2,1)}), bf16[32,32,384]{2,1,0:T(8,128)(2,1)S(1)}, u32[]{:S(2)}, u32[]{:S(2)}) %all-to-all-start.4) | async-done | bytes 786464 | tf_op jit(solution)/shard_map/all_to_all | solution.py:10
  121.7 4.7 %all-to-all-start = ((bf16[10,16,384]{2,0,1:T(8,128)(2,1)}), bf16[10,16,384]{2,0,1:T(8,128)(2,1)S(1)}, u32[]{:S(2)}, u32[]{:S(2)}) async-start(bf16[10,16,384]{2,0,1:T(8,128)(2,1)} %copy.47), calls=%async_computation | async-start | bytes 393216 | tf_op jit(solution)/shard_map/all_to_all | solution.py:56
  128.4 6.3 %all-to-all-done = bf16[10,16,384]{2,0,1:T(8,128)(2,1)S(1)} async-done(((bf16[10,16,384]{2,0,1:T(8,128)(2,1)}), bf16[10,16,384]{2,0,1:T(8,128)(2,1)S(1)}, u32[]{:S(2)}, u32[]{:S(2)}) %all-to-all-start) | async-done | bytes 122912 | tf_op jit(solution)/shard_map/all_to_all | solution.py:56
  134.7 9.1 %all-to-all-start.6 = ((f32[32,1,192]{2,1,0:T(1,128)}), f32[32,1,192]{2,1,0:T(1,128)S(1)}, u32[]{:S(2)}, u32[]{:S(2)}) async-start(f32[32,1,192]{2,1,0:T(1,128)} %reshape.84), calls=%async_computation.6 | async-start | bytes 65536 | tf_op jit(solution)/shard_map/all_to_all | solution.py:79
  146.9 8.7 %all-to-all-done.6 = f32[32,1,192]{2,1,0:T(1,128)S(1)} async-done(((f32[32,1,192]{2,1,0:T(1,128)}), f32[32,1,192]{2,1,0:T(1,128)S(1)}, u32[]{:S(2)}, u32[]{:S(2)}) %all-to-all-start.6) | async-done | bytes 24608 | tf_op jit(solution)/shard_map/all_to_all | solution.py:79
  155.6 4.5 %all-to-all-start.8 = ((bf16[32,32,384]{2,1,0:T(8,128)(2,1)}), bf16[32,32,384]{2,1,0:T(8,128)(2,1)S(1)}, u32[]{:S(2)}, u32[]{:S(2)}) async-start(bf16[32,32,384]{2,1,0:T(8,128)(2,1)} %convert_element_type.30), calls=%async_computation.8 | async-start | bytes 1572864 | tf_op jit(solution)/shard_map/all_to_all | solution.py:80
  163.7 1.8 mul.42
  165.6 22.4 %all-to-all-done.8 = bf16[32,32,384]{2,1,0:T(8,128)(2,1)S(1)} async-done(((bf16[32,32,384]{2,1,0:T(8,128)(2,1)}), bf16[32,32,384]{2,1,0:T(8,128)(2,1)S(1)}, u32[]{:S(2)}, u32[]{:S(2)}) %all-to-all-start.8) | async-done | bytes 786464 | tf_op jit(solution)/shard_map/all_to_all | solution.py:80
  190.4 6.4 %copy.49 = bf16[5120,384]{0,1:T(8,128)(2,1)} copy(bf16[5120,384]{1,0:T(8,128)(2,1)} %all-gather.3.cloned.1.call-done) | data formatting | bytes 7864320 | tf_op jit(solution)/shard_map/all_gather | solution.py:66
  196.7 3.7 %multiply_reduce_fusion = (f32[3,160]{1,0:T(4,128)S(1)}, f32[3,160,5120]{2,1,0:T(8,128)S(1)}) fusion(bf16[5120,3,128]{0,2,1:T(8,128)(2,1)} %bitcast.91, bf16[160,3,128]{2,1,0:T(4,128)(2,1)S(1)} %copy-done.1), kind=kOutput, calls=%fused_computation.1 | convolution fusion | flops 634060288 | bytes 13887360 | tf_op jit(solution)/shard_map/qhd,khd->hqk/dot_general | solution.py:22
  200.4 1.8 fusion
  202.2 2.0 copy-done
  204.2 59.5 %all-gather.5.cloned.1.call-done = bf16[5120,384]{1,0:T(8,128)(2,1)} async-done(((bf16[160,384]{1,0:T(8,128)(2,1)}), bf16[5120,384]{1,0:T(8,128)(2,1)}) %all-gather.5.cloned.1.call-update) | async-done | bytes 3932176 | tf_op jit(solution)/shard_map/all_gather | solution.py:67
  263.7 6.4 %copy.53 = bf16[5120,384]{0,1:T(8,128)(2,1)} copy(bf16[5120,384]{1,0:T(8,128)(2,1)} %all-gather.5.cloned.1.call-done) | data formatting | bytes 7864320 | tf_op jit(solution)/shard_map/all_gather | solution.py:67
  270.0 6.9 %fusion.21 = bf16[3,20,8,128]{3,2,1,0:T(8,128)(2,1)S(1)} fusion(bf16[5120,3,128]{0,2,1:T(8,128)(2,1)} %bitcast.92, f32[3,160,5120]{2,1,0:T(8,128)} %copy-done, f32[3,160]{1,0:T(4,128)S(1)} %get-tuple-element.9, f32[160,3]{0,1:T(4,128)S(1)} %bitcast_add_fusion.2, f32[160,3]{0,1:T(4,128)S(1)} %get-tuple-element.8), kind=kOutput, calls=%fused_computation.18 | convolution fusion | flops 636702720 | bytes 13891200 | tf_op jit(solution)/shard_map/hqk,khd->qhd/dot_general | solution.py:29
  (61 shorter events, 19.7 us)
Async XLA Ops:
  7.2 49.6 %copy-start.2 = (bf16[10,6144]{1,0:T(8,128)(2,1)S(1)}, bf16[10,6144]{1,0:T(8,128)(2,1)}, u32[]{:S(2)}) copy-start(bf16[10,6144]{1,0:T(8,128)(2,1)} %param.11) | copy-start | bytes 368644
  7.2 183.2 %all-gather.3.cloned.1.call-start = ((), (), s32[]{:S(2)}) async-start(), calls=%async_computation.9 | async-start | bytes 4055040 | tf_op jit(solution)/shard_map/all_gather | solution.py:66
  8.3 87.6 %copy-start.3 = (bf16[10,6144]{1,0:T(8,128)(2,1)S(1)}, bf16[10,6144]{1,0:T(8,128)(2,1)}, u32[]{:S(2)}) copy-start(bf16[10,6144]{1,0:T(8,128)(2,1)} %param.6) | copy-start | bytes 368644
  27.8 235.9 %all-gather.5.cloned.1.call-start = ((), (), s32[]{:S(2)}) async-start(), calls=%async_computation.10 | async-start | bytes 4055040 | tf_op jit(solution)/shard_map/all_gather | solution.py:67
  42.0 11.2 %all-to-all-start.3 = ((bf16[2,16,384]{2,0,1:T(2,128)(2,1)}), bf16[2,16,384]{2,0,1:T(2,128)(2,1)S(1)}, u32[]{:S(2)}, u32[]{:S(2)}) async-start(bf16[2,16,384]{2,0,1:T(2,128)(2,1)} %bitcast.115), calls=%async_computation.3 | async-start | bytes 49152 | tf_op jit(solution)/shard_map/all_to_all | solution.py:59
  53.2 11.8 %all-to-all-start.5 = ((bf16[10,16,384]{2,0,1:T(8,128)(2,1)}), bf16[10,16,384]{2,0,1:T(8,128)(2,1)S(1)}, u32[]{:S(2)}, u32[]{:S(2)}) async-start(bf16[10,16,384]{2,0,1:T(8,128)(2,1)} %copy.57), calls=%async_computation.5 | async-start | bytes 393216 | tf_op jit(solution)/shard_map/all_to_all | solution.py:60
  65.0 11.8 %all-to-all-start.7 = ((bf16[10,16,384]{2,0,1:T(8,128)(2,1)}), bf16[10,16,384]{2,0,1:T(8,128)(2,1)S(1)}, u32[]{:S(2)}, u32[]{:S(2)}) async-start(bf16[10,16,384]{2,0,1:T(8,128)(2,1)} %copy.63), calls=%async_computation.7 | async-start | bytes 393216 | tf_op jit(solution)/shard_map/all_to_all | solution.py:61
  77.8 43.9 %all-to-all-start.4 = ((bf16[32,32,384]{2,1,0:T(8,128)(2,1)}), bf16[32,32,384]{2,1,0:T(8,128)(2,1)S(1)}, u32[]{:S(2)}, u32[]{:S(2)}) async-start(bf16[32,32,384]{2,1,0:T(8,128)(2,1)} %stack.11), calls=%async_computation.4 | async-start | bytes 1572864 | tf_op jit(solution)/shard_map/all_to_all | solution.py:10
  121.7 13.0 %all-to-all-start = ((bf16[10,16,384]{2,0,1:T(8,128)(2,1)}), bf16[10,16,384]{2,0,1:T(8,128)(2,1)S(1)}, u32[]{:S(2)}, u32[]{:S(2)}) async-start(bf16[10,16,384]{2,0,1:T(8,128)(2,1)} %copy.47), calls=%async_computation | async-start | bytes 393216 | tf_op jit(solution)/shard_map/all_to_all | solution.py:56
  134.7 20.9 %all-to-all-start.6 = ((f32[32,1,192]{2,1,0:T(1,128)}), f32[32,1,192]{2,1,0:T(1,128)S(1)}, u32[]{:S(2)}, u32[]{:S(2)}) async-start(f32[32,1,192]{2,1,0:T(1,128)} %reshape.84), calls=%async_computation.6 | async-start | bytes 65536 | tf_op jit(solution)/shard_map/all_to_all | solution.py:79
  155.6 32.5 %all-to-all-start.8 = ((bf16[32,32,384]{2,1,0:T(8,128)(2,1)}), bf16[32,32,384]{2,1,0:T(8,128)(2,1)S(1)}, u32[]{:S(2)}, u32[]{:S(2)}) async-start(bf16[32,32,384]{2,1,0:T(8,128)(2,1)} %convert_element_type.30), calls=%async_computation.8 | async-start | bytes 1572864 | tf_op jit(solution)/shard_map/all_to_all | solution.py:80
  190.4 6.4 %copy-start.1 = (bf16[160,3,128]{2,1,0:T(4,128)(2,1)S(1)}, bf16[160,3,128]{2,1,0:T(4,128)(2,1)}, u32[]{:S(2)}) copy-start(bf16[160,3,128]{2,1,0:T(4,128)(2,1)} %reshape.77) | copy-start | bytes 368644
  200.4 3.8 %copy-start = (f32[3,160,5120]{2,1,0:T(8,128)}, f32[3,160,5120]{2,1,0:T(8,128)S(1)}, u32[]{:S(2)}) copy-start(f32[3,160,5120]{2,1,0:T(8,128)S(1)} %get-tuple-element.11) | copy-start | bytes 29491204
Sparse Core Ops, SparseCore 0:
  27.9 124.7 all-gather.2
  156.6 107.0 all-gather.4
